TPU v7x, 256 devices: a whole 4x4x8 slice. The times are simulated.
256 devices in a mesh: row: 8 (over y, core), col: 32 (over z, x).
Axes of the slice: x: 4, y: 4, z: 8, core: 2. Of those that a mesh axis runs over, the one named last changes fastest.
Arguments:
- diag_block: float32 [1024, 1024], P('row')
- panel: bfloat16 [64, 1024, 1024], P('col', 'row'), may hold values from -1 to 1
- trailing: bfloat16 [32, 12, 1024, 1024], P('col', None, 'row'), may hold values from -6 to 6
- slot_rows: int32 [32, 12], replicated, may hold values from -1 to 63, as said below
- slot_cols: int32 [32, 12], replicated, may hold values from 0 to 1, as said below
Outputs:
- panel_factor: bfloat16 [64, 1024, 1024], P('col', 'row')
- updated: bfloat16 [32, 12, 1024, 1024], P('col', None, 'row')
Inputs may be any that keep to these rules, and one draw needn't show every extreme that they name: Slot s of grid column c holds the tile at tile row slot_rows[c, s] and tile column 2 * c + slot_cols[c, s] of the trailing matrix, or nothing where slot_rows[c, s] is -1. Live slots come first in each column; the pairs of one column are distinct and lie on or below the diagonal (tile row at least tile column). Within one grid column, live slots whose tile rows a and a' have a // 2 == a' // 2 have a == a'. Every column holds at least one live slot, column 0 fills all 12 slots and column 16 holds exactly one. `slot_cols`: 0 in empty slots.
All inputs are finite; a program needn't handle non-finite values.
Results may differ from a plain program's by a relative error of at most 0.0019.
Values may be sent and summed in bfloat16 or wider, within the bound.
No kernel may reach another device: no remote copies, remote signals or barrier semaphores. Data moves between devices by JAX's collectives and lax.ppermute only.
A program may use at most 128 MiB of HBM per device.

v0:
```python
import jax
import jax.numpy as jnp
from jax import lax
from jax.sharding import PartitionSpec as P


def slot_product(slices, left_ids, source_tiles, col_ids, position):
    left_slice = lax.dynamic_index_in_dim(slices, left_ids[position], 0, keepdims=False)
    right_tile = lax.dynamic_index_in_dim(source_tiles, col_ids[position], 0, keepdims=False)
    return lax.dot_general(
        left_slice, right_tile, (((1,), (1,)), ((), ())), preferred_element_type=jnp.float32
    )


def subtract_slot(buffer, position, update):
    previous = lax.dynamic_index_in_dim(buffer, position, 0, keepdims=False).astype(jnp.float32)
    return lax.dynamic_update_index_in_dim(
        buffer, (previous - update).astype(jnp.bfloat16), position, 0
    )


def local(diag_block, panel, trailing, slot_rows, slot_cols):
    diag_full = lax.all_gather(diag_block, "row", axis=0, tiled=True)
    factor = jnp.linalg.cholesky(diag_full)
    tile_count, row_count, tile_width = panel.shape
    stacked = panel.astype(jnp.float32).reshape(tile_count * row_count, tile_width)
    solved = lax.linalg.triangular_solve(factor, stacked.T, left_side=True, lower=True)
    panel_factor = solved.T.reshape(tile_count, row_count, tile_width).astype(jnp.bfloat16)
    whole_tiles = lax.all_gather(panel_factor, "row", axis=1, tiled=True)
    column_index = lax.axis_index("col")
    own_rows = lax.dynamic_index_in_dim(slot_rows, column_index, 0, keepdims=False)
    own_cols = lax.dynamic_index_in_dim(slot_cols, column_index, 0, keepdims=False)
    own_count = jnp.sum((own_rows >= 0).astype(jnp.int32))
    slices = lax.all_gather(panel_factor, "col", axis=0, tiled=True)

    def own_step(position, buffer):
        return subtract_slot(
            buffer, position, slot_product(slices, own_rows, whole_tiles, own_cols, position)
        )

    buffer = lax.fori_loop(0, own_count, own_step, trailing[0])
    return (panel_factor, buffer[None])


def solution(mesh):
    return jax.shard_map(
        local,
        mesh=mesh,
        in_specs=(P("row", None), P("col", "row", None), P("col", None, "row", None), P(), P()),
        out_specs=(P("col", "row", None), P("col", None, "row", None)),
        check_vma=False,
    )
```

profile of v0, /device:TPU:1, one launch (start us, length us, event | category | flops | bytes accessed | tf_op | source)
XLA Modules:
  0.0 681.8 jit_solution(6531067428901336610)
XLA Ops:
  9.6 43.7 %all-gather.4.cloned.1.call-done = f32[1024,1024]{0,1:T(8,128)} async-done(((f32[128,1024]{0,1:T(8,128)}), f32[1024,1024]{0,1:T(8,128)}) %all-gather.4.cloned.1.call-update) | async-done | bytes 4194320 | tf_op jit(solution)/shard_map/all_gather | solution.py:23
  53.3 5.3 copy.18
  58.7 4.4 fusion.18
  65.0 11.7 %cholesky.223 = f32[128,128]{1,0:T(8,128)S(1)} custom-call(f32[128,128]{1,0:T(8,128)S(1)} %cholesky.580), custom_call_target="Cholesky" | custom-call | tf_op jit(solution)/shard_map/jit(cholesky)/cholesky | solution.py:24
  76.8 9.8 %custom-call.62 = f32[1,128,128]{1,2,0:T(8,128)S(1)} custom-call(f32[1,128,128]{2,1,0:T(8,128)S(1)} %get-tuple-element.117), custom_call_target="InvertDiagBlocksLowerTriangular" | custom-call | tf_op jit(solution)/shard_map/jit(cholesky)/cholesky | solution.py:24
  93.0 12.2 %cholesky.244 = f32[128,128]{1,0:T(8,128)S(1)} custom-call(f32[128,128]{1,0:T(8,128)S(1)} %cholesky.584), custom_call_target="Cholesky" | custom-call | tf_op jit(solution)/shard_map/jit(cholesky)/cholesky | solution.py:24
  105.8 9.8 %custom-call.63 = f32[1,128,128]{1,2,0:T(8,128)S(1)} custom-call(f32[1,128,128]{2,1,0:T(8,128)S(1)} %get-tuple-element.114), custom_call_target="InvertDiagBlocksLowerTriangular" | custom-call | tf_op jit(solution)/shard_map/jit(cholesky)/cholesky | solution.py:24
  119.0 11.7 %cholesky.468 = f32[128,128]{1,0:T(8,128)S(1)} custom-call(f32[128,128]{1,0:T(8,128)S(1)} %cholesky.589), custom_call_target="Cholesky" | custom-call | tf_op jit(solution)/shard_map/jit(cholesky)/cholesky | solution.py:24
  132.0 9.8 %custom-call.64 = f32[1,128,128]{1,2,0:T(8,128)S(1)} custom-call(f32[1,128,128]{2,1,0:T(8,128)S(1)} %get-tuple-element.111), custom_call_target="InvertDiagBlocksLowerTriangular" | custom-call | tf_op jit(solution)/shard_map/jit(cholesky)/cholesky | solution.py:24
  145.3 11.8 %cholesky.487 = f32[128,128]{1,0:T(8,128)S(1)} custom-call(f32[128,128]{1,0:T(8,128)S(1)} %cholesky.594), custom_call_target="Cholesky" | custom-call | tf_op jit(solution)/shard_map/jit(cholesky)/cholesky | solution.py:24
  158.5 9.8 %custom-call.65 = f32[1,128,128]{1,2,0:T(8,128)S(1)} custom-call(f32[1,128,128]{2,1,0:T(8,128)S(1)} %get-tuple-element.108), custom_call_target="InvertDiagBlocksLowerTriangular" | custom-call | tf_op jit(solution)/shard_map/jit(cholesky)/cholesky | solution.py:24
  171.7 11.7 %cholesky.506 = f32[128,128]{1,0:T(8,128)S(1)} custom-call(f32[128,128]{1,0:T(8,128)S(1)} %cholesky.599), custom_call_target="Cholesky" | custom-call | tf_op jit(solution)/shard_map/jit(cholesky)/cholesky | solution.py:24
  184.7 10.0 %custom-call.66 = f32[1,128,128]{1,2,0:T(8,128)S(1)} custom-call(f32[1,128,128]{2,1,0:T(8,128)S(1)} %get-tuple-element.105), custom_call_target="InvertDiagBlocksLowerTriangular" | custom-call | tf_op jit(solution)/shard_map/jit(cholesky)/cholesky | solution.py:24
  198.1 11.7 %cholesky.526 = f32[128,128]{1,0:T(8,128)S(1)} custom-call(f32[128,128]{1,0:T(8,128)S(1)} %cholesky.604), custom_call_target="Cholesky" | custom-call | tf_op jit(solution)/shard_map/jit(cholesky)/cholesky | solution.py:24
  211.0 9.8 %custom-call.67 = f32[1,128,128]{1,2,0:T(8,128)S(1)} custom-call(f32[1,128,128]{2,1,0:T(8,128)S(1)} %get-tuple-element.102), custom_call_target="InvertDiagBlocksLowerTriangular" | custom-call | tf_op jit(solution)/shard_map/jit(cholesky)/cholesky | solution.py:24
  223.8 12.1 %cholesky.546 = f32[128,128]{1,0:T(8,128)S(1)} custom-call(f32[128,128]{1,0:T(8,128)S(1)} %cholesky.609), custom_call_target="Cholesky" | custom-call | tf_op jit(solution)/shard_map/jit(cholesky)/cholesky | solution.py:24
  237.2 9.8 %custom-call.68 = f32[1,128,128]{1,2,0:T(8,128)S(1)} custom-call(f32[1,128,128]{2,1,0:T(8,128)S(1)} %get-tuple-element.99), custom_call_target="InvertDiagBlocksLowerTriangular" | custom-call | tf_op jit(solution)/shard_map/jit(cholesky)/cholesky | solution.py:24
  249.7 11.7 %cholesky.564 = f32[128,128]{1,0:T(8,128)S(1)} custom-call(f32[128,128]{1,0:T(8,128)S(1)} %convolution_subtract_fusion.13), custom_call_target="Cholesky" | custom-call | tf_op jit(solution)/shard_map/jit(cholesky)/cholesky | solution.py:24
  268.3 4.8 select_select_fusion
  273.1 23.0 %while.12 = (s32[]{:T(128)}, f32[1024,1024]{1,0:T(8,128)}, s32[8,2]{0,1:T(2,128)S(1)}, f32[8,128,128]{2,1,0:T(8,128)S(1)}, s32[]{:T(128)}) while((s32[]{:T(128)}, f32[1024,1024]{1,0:T(8,128)}, s32[8,2]{0,1:T(2,128)S(1)}, f32[8,128,128]{2,1,0:T(8,128)S(1)}, s32[]{:T(128)}) %tuple.74), condition=%wide.while_cond, body=%wide.while_body.sunk | while | flops 2 | bytes 131189 | solution.py:27
  296.1 78.8 %custom-call.69 = f32[8,128,128]{1,2,0:T(8,128)S(1)} custom-call(f32[8,128,128]{2,1,0:T(8,128)S(1)} %get-tuple-element.48), custom_call_target="InvertDiagBlocksLowerTriangular" | custom-call | tf_op jit(solution)/shard_map/triangular_solve | solution.py:27
  398.6 34.2 %all-gather.8.cloned.1.call-done = bf16[2,1024,1024]{2,1,0:T(8,128)(2,1)} async-done(((bf16[2,128,1024]{2,1,0:T(8,128)(2,1)}), bf16[2,1024,1024]{2,1,0:T(8,128)(2,1)}) %all-gather.8.cloned.1.call-update) | async-done | bytes 4194320 | tf_op jit(solution)/shard_map/all_gather | solution.py:29
  432.8 142.9 %all-gather.6.cloned.1.call-done = bf16[64,128,1024]{2,1,0:T(8,128)(2,1)} async-done(((bf16[2,128,1024]{2,1,0:T(8,128)(2,1)}), bf16[64,128,1024]{2,1,0:T(8,128)(2,1)}) %all-gather.6.cloned.1.call-update) | async-done | bytes 16777232 | tf_op jit(solution)/shard_map/all_gather | solution.py:34
  575.8 97.6 %while.11 = (s32[]{:T(128)}, bf16[12,128,1024]{2,1,0:T(8,128)(2,1)S(1)}, s32[]{:T(128)}, s32[12]{0:T(128)S(1)}, bf16[64,128,1024]{2,1,0:T(8,128)(2,1)}, /*index=...) while((s32[]{:T(128)}, ...), condition=%wide.region_18.19_spmd, body=%wide.region_17.18_spmd.sunk | while | flops 268828672 | bytes 3408139 | solution.py:41
  (164 shorter events, 132.0 us)
Async XLA Ops:
  7.2 1.0 copy-start.4
  7.2 2.1 copy-start.5
  7.2 46.1 %all-gather.4.cloned.1.call-start = ((), (), s32[]{:S(2)}) async-start(), calls=%async_computation | async-start | bytes 4718592 | tf_op jit(solution)/shard_map/all_gather | solution.py:23
  9.2 423.6 %all-gather.8.cloned.1.call-start = ((), (), s32[]{:S(2)}) async-start(), calls=%async_computation.2 | async-start | bytes 4718592 | tf_op jit(solution)/shard_map/all_gather | solution.py:29
  9.6 372.6 %copy-start.3 = (f32[1024,256]{1,0:T(8,128)}, f32[1024,256]{1,0:T(8,128)S(1)}, u32[]{:S(2)}) copy-start(f32[1024,256]{1,0:T(8,128)S(1)} %bitcast_convert_fusion) | copy-start | bytes 3145732
  63.1 1.9 copy-start
  374.9 9.7 %copy-start.6 = (f32[8,128,128]{1,2,0:T(8,128)}, f32[8,128,128]{1,2,0:T(8,128)S(1)}, u32[]{:S(2)}) copy-start(f32[8,128,128]{1,2,0:T(8,128)S(1)} %custom-call.69) | copy-start | bytes 1572868
  384.7 13.1 %copy-start.7 = (s32[32,12]{0,1:T(8,128)S(1)}, s32[32,12]{0,1:T(8,128)}, u32[]{:S(2)}) copy-start(s32[32,12]{0,1:T(8,128)} %param.11) | copy-start | bytes 4612
  384.7 13.1 %copy-start.8 = (s32[32,12]{0,1:T(8,128)S(1)}, s32[32,12]{0,1:T(8,128)}, u32[]{:S(2)}) copy-start(s32[32,12]{0,1:T(8,128)} %param.10) | copy-start | bytes 4612
  384.7 191.1 %copy-start.2 = (bf16[1,12,128,1024]{3,2,1,0:T(8,128)(2,1)S(1)}, bf16[1,12,128,1024]{3,2,1,0:T(8,128)(2,1)}, u32[]{:S(2)}) copy-start(bf16[1,12,128,1024]{3,2,1,0:T(8,128)(2,1)} %param.9) | copy-start | bytes 9437188
  397.0 178.7 %all-gather.6.cloned.1.call-start = ((), (), s32[]{:S(2)}) async-start(), calls=%async_computation.1 | async-start | bytes 17301504 | tf_op jit(solution)/shard_map/all_gather | solution.py:34
  673.4 1.7 copy-start.1
Sparse Core Ops, SparseCore 0:
  10.4 42.8 all-gather.3
  397.1 35.6 all-gather.7
  436.0 139.6 all-gather.5
where the time goes:
time: 693 us; the launch traced here: 682 us
  other arithmetic  261 us (38%)
  waiting for transfers between devices  222 us (32%)
  matrix products  73.2 us (11%)
  local copies, waits for them, and re-layouts  53.5 us (8%)
  loops' own time  52.9 us (8%)
  between operations  19.3 us (3%)
    another operation x30, other arithmetic, local(): factor = jnp.linalg.cholesky(diag_full)  173 us
    all_gather x1, waiting for transfers between devices, local(): slices = lax.all_gather(panel_factor, 'col', axis=0, tiled=True)  143 us
    another operation x3, other arithmetic, local(): lax.linalg.triangular_solve(factor, stacked.T, left_side=True, lower=True)  83.6 us
    another operation x1, loops' own time, local(): buffer = lax.fori_loop(0, own_count, own_step, trailing[0])  52.7 us
    all_gather x1, waiting for transfers between devices, local(): diag_full = lax.all_gather(diag_block, 'row', axis=0, tiled=True)  43.7 us
    all_gather x1, waiting for transfers between devices, local(): whole_tiles = lax.all_gather(panel_factor, 'row', axis=1, tiled=True)  34.2 us
    dot_general x12, matrix products, slot_product(): lax.dot_general(left_slice, right_tile, (((1,), (1,)), ((), ())), preferr...  30.3 us
    another operation x14, matrix products, local(): factor = jnp.linalg.cholesky(diag_full)  23.1 us
  transfers between devices with their start and end apart: 3, of which 3 were waited for; matrix products, arithmetic and copies ran while one was open for 0% of the time, Pallas kernels for 0%

commit v1 on v0

--- a/solution.py
+++ b/solution.py
@@ -26,7 +26,10 @@
     stacked = panel.astype(jnp.float32).reshape(tile_count * row_count, tile_width)
     solved = lax.linalg.triangular_solve(factor, stacked.T, left_side=True, lower=True)
     panel_factor = solved.T.reshape(tile_count, row_count, tile_width).astype(jnp.bfloat16)
-    whole_tiles = lax.all_gather(panel_factor, "row", axis=1, tiled=True)
+    n_dev = lax.axis_size("row")
+    blocks = jnp.stack([panel_factor for _ in range(n_dev)])
+    blocks = lax.all_to_all(blocks, "row", split_axis=0, concat_axis=0)
+    whole_tiles = jnp.concatenate(blocks, axis=1)
     column_index = lax.axis_index("col")
     own_rows = lax.dynamic_index_in_dim(slot_rows, column_index, 0, keepdims=False)
     own_cols = lax.dynamic_index_in_dim(slot_cols, column_index, 0, keepdims=False)

time: 693 us -> 647 us (0.934)
  waiting for transfers between devices: 222 us -> 171 us
  matrix products: 73.2 us -> 65.4 us
  local copies, waits for them, and re-layouts: 53.5 us -> 61.3 us
    all_gather x1, waiting for transfers between devices: 143 us -> 78.9 us  [local(): slices = lax.all_gather(panel_factor, 'col', axis=0, tiled=True)]
    all_to_all x0 -> x1, waiting for transfers between devices: none -> 48.1 us  [local(): blocks = lax.all_to_all(blocks, 'row', split_axis=0, concat_axis=0)]
    all_gather x1 -> x0, waiting for transfers between devices: 34.2 us -> none  [local(): whole_tiles = lax.all_gather(panel_factor, 'row', axis=1, tiled=True)]
    another operation x15, matrix products: 19.7 us -> 12 us  [local(): lax.linalg.triangular_solve(factor, stacked.T, left_side=True, lower=True)]
    another operation x24 -> x25, local copies, waits for them, and re-layouts: 22.8 us -> 26.3 us
  transfers between devices with their start and end apart: 3 -> 3, of which waited for: 3 -> 3; matrix products, arithmetic and copies ran while one was open for 0% -> 1% of each run, Pallas kernels for 0% -> 0%
where the time goes in v1:
time: 647 us; the launch traced here: 636 us
  other arithmetic  261 us (40%)
  waiting for transfers between devices  171 us (26%)
  matrix products  65.4 us (10%)
  local copies, waits for them, and re-layouts  61.3 us (9%)
  loops' own time  52.7 us (8%)
  between operations  19.5 us (3%)
    another operation x30, other arithmetic, local(): factor = jnp.linalg.cholesky(diag_full)  172 us
    another operation x3, other arithmetic, local(): lax.linalg.triangular_solve(factor, stacked.T, left_side=True, lower=True)  83.6 us
    all_gather x1, waiting for transfers between devices, local(): slices = lax.all_gather(panel_factor, 'col', axis=0, tiled=True)  78.9 us
    another operation x1, loops' own time, local(): buffer = lax.fori_loop(0, own_count, own_step, trailing[0])  52.5 us
    all_to_all x1, waiting for transfers between devices, local(): blocks = lax.all_to_all(blocks, 'row', split_axis=0, concat_axis=0)  48.1 us
    all_gather x1, waiting for transfers between devices, local(): diag_full = lax.all_gather(diag_block, 'row', axis=0, tiled=True)  43.7 us
    dot_general x12, matrix products, slot_product(): lax.dot_general(left_slice, right_tile, (((1,), (1,)), ((), ())), preferr...  30.3 us
    another operation x14, matrix products, local(): factor = jnp.linalg.cholesky(diag_full)  23.1 us
  transfers between devices with their start and end apart: 3, of which 3 were waited for; matrix products, arithmetic and copies ran while one was open for 1% of the time, Pallas kernels for 0%

profile of v1, /device:TPU:1, one launch (start us, length us, event | category | flops | bytes accessed | tf_op | source)
XLA Modules:
  0.0 635.8 jit_solution(16033865440396362444)
XLA Ops:
  9.6 43.7 %all-gather.3.cloned.1.call-done = f32[1024,1024]{0,1:T(8,128)} async-done(((f32[128,1024]{0,1:T(8,128)}), f32[1024,1024]{0,1:T(8,128)}) %all-gather.3.cloned.1.call-update) | async-done | bytes 4194320 | tf_op jit(solution)/shard_map/all_gather | solution.py:23
  53.3 5.3 copy.24
  65.0 11.7 %cholesky.223 = f32[128,128]{1,0:T(8,128)S(1)} custom-call(f32[128,128]{1,0:T(8,128)S(1)} %cholesky.580), custom_call_target="Cholesky" | custom-call | tf_op jit(solution)/shard_map/jit(cholesky)/cholesky | solution.py:24
  76.8 9.8 %custom-call.62 = f32[1,128,128]{1,2,0:T(8,128)S(1)} custom-call(f32[1,128,128]{2,1,0:T(8,128)S(1)} %get-tuple-element.119), custom_call_target="InvertDiagBlocksLowerTriangular" | custom-call | tf_op jit(solution)/shard_map/jit(cholesky)/cholesky | solution.py:24
  93.0 12.2 %cholesky.244 = f32[128,128]{1,0:T(8,128)S(1)} custom-call(f32[128,128]{1,0:T(8,128)S(1)} %cholesky.584), custom_call_target="Cholesky" | custom-call | tf_op jit(solution)/shard_map/jit(cholesky)/cholesky | solution.py:24
  105.8 9.8 %custom-call.63 = f32[1,128,128]{1,2,0:T(8,128)S(1)} custom-call(f32[1,128,128]{2,1,0:T(8,128)S(1)} %get-tuple-element.116), custom_call_target="InvertDiagBlocksLowerTriangular" | custom-call | tf_op jit(solution)/shard_map/jit(cholesky)/cholesky | solution.py:24
  119.0 11.7 %cholesky.468 = f32[128,128]{1,0:T(8,128)S(1)} custom-call(f32[128,128]{1,0:T(8,128)S(1)} %cholesky.589), custom_call_target="Cholesky" | custom-call | tf_op jit(solution)/shard_map/jit(cholesky)/cholesky | solution.py:24
  132.0 9.8 %custom-call.64 = f32[1,128,128]{1,2,0:T(8,128)S(1)} custom-call(f32[1,128,128]{2,1,0:T(8,128)S(1)} %get-tuple-element.113), custom_call_target="InvertDiagBlocksLowerTriangular" | custom-call | tf_op jit(solution)/shard_map/jit(cholesky)/cholesky | solution.py:24
  145.3 11.8 %cholesky.487 = f32[128,128]{1,0:T(8,128)S(1)} custom-call(f32[128,128]{1,0:T(8,128)S(1)} %cholesky.594), custom_call_target="Cholesky" | custom-call | tf_op jit(solution)/shard_map/jit(cholesky)/cholesky | solution.py:24
  158.4 9.8 %custom-call.65 = f32[1,128,128]{1,2,0:T(8,128)S(1)} custom-call(f32[1,128,128]{2,1,0:T(8,128)S(1)} %get-tuple-element.110), custom_call_target="InvertDiagBlocksLowerTriangular" | custom-call | tf_op jit(solution)/shard_map/jit(cholesky)/cholesky | solution.py:24
  171.7 11.7 %cholesky.506 = f32[128,128]{1,0:T(8,128)S(1)} custom-call(f32[128,128]{1,0:T(8,128)S(1)} %cholesky.599), custom_call_target="Cholesky" | custom-call | tf_op jit(solution)/shard_map/jit(cholesky)/cholesky | solution.py:24
  184.7 10.0 %custom-call.66 = f32[1,128,128]{1,2,0:T(8,128)S(1)} custom-call(f32[1,128,128]{2,1,0:T(8,128)S(1)} %get-tuple-element.107), custom_call_target="InvertDiagBlocksLowerTriangular" | custom-call | tf_op jit(solution)/shard_map/jit(cholesky)/cholesky | solution.py:24
  198.0 11.7 %cholesky.526 = f32[128,128]{1,0:T(8,128)S(1)} custom-call(f32[128,128]{1,0:T(8,128)S(1)} %cholesky.604), custom_call_target="Cholesky" | custom-call | tf_op jit(solution)/shard_map/jit(cholesky)/cholesky | solution.py:24
  211.0 9.8 %custom-call.67 = f32[1,128,128]{1,2,0:T(8,128)S(1)} custom-call(f32[1,128,128]{2,1,0:T(8,128)S(1)} %get-tuple-element.104), custom_call_target="InvertDiagBlocksLowerTriangular" | custom-call | tf_op jit(solution)/shard_map/jit(cholesky)/cholesky | solution.py:24
  223.8 12.1 %cholesky.546 = f32[128,128]{1,0:T(8,128)S(1)} custom-call(f32[128,128]{1,0:T(8,128)S(1)} %cholesky.609), custom_call_target="Cholesky" | custom-call | tf_op jit(solution)/shard_map/jit(cholesky)/cholesky | solution.py:24
  237.1 9.8 %custom-call.68 = f32[1,128,128]{1,2,0:T(8,128)S(1)} custom-call(f32[1,128,128]{2,1,0:T(8,128)S(1)} %get-tuple-element.101), custom_call_target="InvertDiagBlocksLowerTriangular" | custom-call | tf_op jit(solution)/shard_map/jit(cholesky)/cholesky | solution.py:24
  249.6 11.7 %cholesky.564 = f32[128,128]{1,0:T(8,128)S(1)} custom-call(f32[128,128]{1,0:T(8,128)S(1)} %convolution_subtract_fusion.13), custom_call_target="Cholesky" | custom-call | tf_op jit(solution)/shard_map/jit(cholesky)/cholesky | solution.py:24
  268.1 4.8 select_select_fusion
  272.9 23.0 %while.12 = (s32[]{:T(128)}, f32[1024,1024]{1,0:T(8,128)}, s32[8,2]{0,1:T(2,128)S(1)}, f32[8,128,128]{2,1,0:T(8,128)S(1)}, s32[]{:T(128)}) while((s32[]{:T(128)}, f32[1024,1024]{1,0:T(8,128)}, s32[8,2]{0,1:T(2,128)S(1)}, f32[8,128,128]{2,1,0:T(8,128)S(1)}, s32[]{:T(128)}) %tuple.75), condition=%wide.while_cond, body=%wide.while_body.sunk | while | flops 2 | bytes 131181 | solution.py:27
  295.9 78.8 %custom-call.69 = f32[8,128,128]{1,2,0:T(8,128)S(1)} custom-call(f32[8,128,128]{2,1,0:T(8,128)S(1)} %get-tuple-element.48), custom_call_target="InvertDiagBlocksLowerTriangular" | custom-call | tf_op jit(solution)/shard_map/triangular_solve | solution.py:27
  391.6 4.8 all-to-all-start
  397.2 48.1 %all-to-all-done = bf16[8,2,128,1024]{3,2,1,0:T(8,128)(2,1)} async-done(((bf16[8,2,128,1024]{3,2,1,0:T(8,128)(2,1)}), bf16[8,2,128,1024]{3,2,1,0:T(8,128)(2,1)}, u32[]{:S(2)}, u32[]{:S(2)}) %all-to-all-start) | async-done | bytes 4194336 | tf_op jit(solution)/shard_map/all_to_all | solution.py:31
  450.0 78.9 %all-gather.5.cloned.1.call-done = bf16[64,128,1024]{2,1,0:T(8,128)(2,1)} async-done(((bf16[2,128,1024]{2,1,0:T(8,128)(2,1)}), bf16[64,128,1024]{2,1,0:T(8,128)(2,1)}) %all-gather.5.cloned.1.call-update) | async-done | bytes 16777232 | tf_op jit(solution)/shard_map/all_gather | solution.py:37
  528.9 98.1 %while.11 = (s32[]{:T(128)}, bf16[12,128,1024]{2,1,0:T(8,128)(2,1)S(1)}, s32[]{:T(128)}, s32[12]{0:T(128)S(1)}, bf16[64,128,1024]{2,1,0:T(8,128)(2,1)}, /*index=...) while((s32[]{:T(128)}, ...), condition=%wide.region_18.19_spmd, body=%wide.region_17.18_spmd.sunk | while | flops 268828672 | bytes 3408131 | solution.py:44
  (161 shorter events, 135.7 us)
Async XLA Ops:
  7.2 1.0 copy-start.3
  7.2 2.1 copy-start.4
  7.2 46.1 %all-gather.3.cloned.1.call-start = ((), (), s32[]{:S(2)}) async-start(), calls=%async_computation.1 | async-start | bytes 4718592 | tf_op jit(solution)/shard_map/all_gather | solution.py:23
  9.2 519.7 %all-gather.5.cloned.1.call-start = ((), (), s32[]{:S(2)}) async-start(), calls=%async_computation.2 | async-start | bytes 17301504 | tf_op jit(solution)/shard_map/all_gather | solution.py:37
  63.1 1.9 copy-start
  391.6 4.8 copy-start.5
  391.6 4.8 copy-start.6
  391.6 53.7 %all-to-all-start = ((bf16[8,2,128,1024]{3,2,1,0:T(8,128)(2,1)}), bf16[8,2,128,1024]{3,2,1,0:T(8,128)(2,1)}, u32[]{:S(2)}, u32[]{:S(2)}) async-start(bf16[8,2,128,1024]{3,2,1,0:T(8,128)(2,1)} %stack.2), calls=%async_computation | async-start | bytes 8388608 | tf_op jit(solution)/shard_map/all_to_all | solution.py:31
  397.2 131.7 %copy-start.2 = (bf16[1,12,128,1024]{3,2,1,0:T(8,128)(2,1)S(1)}, bf16[1,12,128,1024]{3,2,1,0:T(8,128)(2,1)}, u32[]{:S(2)}) copy-start(bf16[1,12,128,1024]{3,2,1,0:T(8,128)(2,1)} %param.9) | copy-start | bytes 9437188
  627.1 1.7 copy-start.1
Sparse Core Ops, SparseCore 0:
  10.4 42.8 all-gather.2
  388.2 140.7 all-gather.4
